TPU v7x, 256 devices: a whole 4x4x8 slice. The times are simulated.
256 devices in a mesh: mem: 16 (over z, core), reg: 16 (over x, y).
Axes of the slice: x: 4, y: 4, z: 8, core: 2. Of those that a mesh axis runs over, the one named last changes fastest.
Arguments:
- anomalies: bfloat16 [1024, 262144], P('mem', 'reg'), may hold values from -6 to 6
- obs_anomalies: bfloat16 [1024, 8192], P('mem', 'reg'), may hold values from -6 to 6
- innovations: bfloat16 [1024, 8192], P('mem', 'reg'), may hold values from -6 to 6
- obs_links: int32 [2048, 12], P('reg'), may hold values from 0 to 19, as said below
- taper_choice: int32 [2048, 12], P('reg'), may hold values from 0 to 7
- tapers: float32 [8, 128, 128], replicated, may hold values from 0.1 to 1
Outputs:
- increments: bfloat16 [1024, 262144], P('mem', 'reg')
Inputs may be any that keep to these rules, and one draw needn't show every extreme that they name: `obs_links`: each row names 12 different positions of a window of 20 observation blocks: position w is block w mod 4 of region r + w // 4 - 2 (regions counted cyclically), r being the state block's region.
All inputs are finite; a program needn't handle non-finite values.
Results may differ from a plain program's by a relative error of at most 0.005.
Values may be sent and summed in bfloat16 or wider, within the bound.
No kernel may reach another device: no remote copies, remote signals or barrier semaphores. Data moves between devices by JAX's collectives and lax.ppermute only.
A program may use at most 128 MiB of HBM per device.

v0:
```python
import jax
import jax.numpy as jnp
from jax import lax
from jax.experimental import pallas as pl
from jax.experimental.pallas import tpu as pltpu
from jax.sharding import PartitionSpec as P

BLK = 128

RING = (0, 1, -1, 2, -2, 3, -3, 4)


def along_z(x, by):
    size = lax.axis_size("mem")
    return lax.ppermute(x, "mem", [(i, (i + 2 * by) % size) for i in range(size)])


def other_core(x):
    size = lax.axis_size("mem")
    return lax.ppermute(x, "mem", [(i, i ^ 1) for i in range(size)])


def along_reg(x, by):
    size = lax.axis_size("reg")
    return lax.ppermute(x, "reg", [(i, (i + by) % size) for i in range(size)])


def gather_other(core_ref, anomalies, out, sems):
    z = core_ref[0]
    core = core_ref[1]
    width = out.shape[-1]
    copies = []
    for j, d in enumerate(RING):
        at = pl.multiple_of((((z + d) & 7) * 2 + (1 - core)) * width, width)
        copies.append(pltpu.make_async_copy(anomalies.at[:, pl.ds(at, width)], out.at[j], sems.at[j]))
    for copy in copies:
        copy.start()
    for copy in copies:
        copy.wait()


def gather_both(core_ref, anomalies, other, *refs):
    outs, sems = refs[:8], refs[8]
    z = core_ref[0]
    core = core_ref[1]
    width = other.shape[-1]
    copies = []
    for j, d in enumerate(RING):
        at = pl.multiple_of((((z + d) & 7) * 2 + core) * width, width)
        copies.append(pltpu.make_async_copy(anomalies.at[:, pl.ds(at, width)], outs[j].at[0], sems.at[j]))
    for copy in copies:
        copy.start()
    for j in range(8):
        outs[j][1] = other[j]
    for copy in copies:
        copy.wait()


def messages(place, anomalies, width):
    rows = anomalies.shape[0]
    smem = pl.BlockSpec(memory_space=pltpu.SMEM)
    vmem = pl.BlockSpec(memory_space=pltpu.VMEM)
    hbm = pl.BlockSpec(memory_space=pltpu.HBM)
    other = pl.pallas_call(
        gather_other,
        out_shape=jax.ShapeDtypeStruct((8, rows, width), jnp.bfloat16),
        in_specs=[smem, hbm],
        out_specs=vmem,
        scratch_shapes=[pltpu.SemaphoreType.DMA((8,))],
        compiler_params=pltpu.CompilerParams(vmem_limit_bytes=4 << 20),
        cost_estimate=pl.CostEstimate(flops=0, bytes_accessed=2 << 20, transcendentals=0),
        name="gather_other",
    )(place, anomalies)
    other = other_core(other)
    return pl.pallas_call(
        gather_both,
        out_shape=[jax.ShapeDtypeStruct((2, rows, width), jnp.bfloat16)] * 8,
        in_specs=[smem, hbm, vmem],
        out_specs=[vmem] * 8,
        scratch_shapes=[pltpu.SemaphoreType.DMA((8,))],
        compiler_params=pltpu.CompilerParams(vmem_limit_bytes=6 << 20),
        cost_estimate=pl.CostEstimate(flops=0, bytes_accessed=4 << 20, transcendentals=0),
        name="gather_both",
    )(place, anomalies, other)


def body(scal, tapers, *refs):
    patches = refs[:8]
    windows = refs[8:28]
    out, held, obs, innov, cols, tapered, scaled, done, in_sems, out_sems = refs[28:]
    z = scal[0]
    core = scal[1]
    width = cols.shape[0]
    slices = obs.shape[1]
    count = obs.shape[-1]
    depth = slices * 64
    copies = [pltpu.make_async_copy(patches[j], held.at[j], in_sems.at[j]) for j in range(8)]
    obs_copies = [
        pltpu.make_async_copy(windows[k].at[:, :, pl.ds(0, count)], obs.at[k], in_sems.at[8 + k]) for k in range(20)
    ]
    innov_copies = [
        pltpu.make_async_copy(windows[k].at[:, :, pl.ds(count, count)], innov.at[k], in_sems.at[28 + k])
        for k in range(20)
    ]
    for copy in copies + obs_copies[:4]:
        copy.start()
    scaled[pl.ds(0, 8)] = tapers[...] * (1.0 / 1023.0)
    scaled[8] = jnp.zeros((BLK, BLK), jnp.float32)
    for k in range(4):
        copies[2 * k].wait()
        copies[2 * k + 1].wait()
        for copy in obs_copies[4 * k + 4 : 4 * k + 8]:
            copy.start()
        for h in range(2):
            pair = jnp.concatenate([held[2 * k, h], held[2 * k + 1, h]], axis=0)
            cols[:, pl.ds((4 * h + k) * BLK, BLK)] = pair.T
    for k in range(4):
        for region in range(5):
            innov_copies[4 * region + k].start()

    for region in range(5):
        for copy in obs_copies[4 * region : 4 * region + 4]:
            copy.wait()
        for half in range(2):
            cov = jnp.zeros((width, 256), jnp.float32)
            for k in range(4):
                y = obs[4 * region + k, :, :, pl.ds(half * 256, 256)].reshape(depth, 256)
                cov += jnp.dot(cols[:, pl.ds(k * depth, depth)], y, preferred_element_type=jnp.float32)
            for b in range(width // BLK):
                for w in range(2):
                    at = region * 512 + half * 256 + w * BLK
                    t = scal[8 + b * 20 + at // BLK]
                    tile = cov[b * BLK : (b + 1) * BLK, w * BLK : (w + 1) * BLK] * scaled[t]
                    tapered[pl.ds(b * BLK, BLK), pl.ds(at, BLK)] = tile.astype(jnp.bfloat16)

    out_copies = []
    for k in range(4):
        for region in range(5):
            innov_copies[4 * region + k].wait()
        for at in range(0, width, 256):
            total = jnp.zeros((depth, 256), jnp.float32)
            for region in range(5):
                total += lax.dot_general(
                    innov[4 * region + k].reshape(depth, count),
                    tapered[pl.ds(at, 256), pl.ds(region * count, count)],
                    (((1,), (1,)), ((), ())),
                    preferred_element_type=jnp.float32,
                )
            done[pl.ds(k * slices, slices), :, pl.ds(at, 256)] = total.astype(jnp.bfloat16).reshape(slices, 64, 256)
        for i in range(slices):
            j, h = (k % 2) * slices + i, k // 2
            copy = pltpu.make_async_copy(
                done.at[k * slices + i], out.at[(z - RING[j]) & 7, core ^ h], out_sems.at[k * slices + i]
            )
            copy.start()
            out_copies.append(copy)
    for copy in out_copies:
        copy.wait()


def analyse(scal, tapers, patches, windows):
    smem = pl.BlockSpec(memory_space=pltpu.SMEM)
    vmem = pl.BlockSpec(memory_space=pltpu.VMEM)
    hbm = pl.BlockSpec(memory_space=pltpu.HBM)
    members, width = patches[0].shape[1:]
    slices = windows[0].shape[0]
    return pl.pallas_call(
        body,
        out_shape=jax.ShapeDtypeStruct((8, 2, members, width), jnp.bfloat16),
        in_specs=[smem, vmem] + [hbm] * 28,
        out_specs=hbm,
        scratch_shapes=[
            pltpu.VMEM((8, 2, members, width), jnp.bfloat16),
            pltpu.VMEM((20, slices, members, 512), jnp.bfloat16),
            pltpu.VMEM((20, slices, members, 512), jnp.bfloat16),
            pltpu.VMEM((width, 1024), jnp.bfloat16),
            pltpu.VMEM((width, 2560), jnp.bfloat16),
            pltpu.VMEM((9, BLK, BLK), jnp.float32),
            pltpu.VMEM((16, members, width), jnp.bfloat16),
            pltpu.SemaphoreType.DMA((48,)),
            pltpu.SemaphoreType.DMA((16,)),
        ],
        compiler_params=pltpu.CompilerParams(vmem_limit_bytes=24 << 20),
        cost_estimate=pl.CostEstimate(flops=11 * 10**9, bytes_accessed=15 << 20, transcendentals=0),
        name="analyse",
    )(scal, tapers, *patches, *windows)


def step(anomalies, obs_anomalies, innovations, obs_links, taper_choice, tapers):
    mem_dev, state_cols = anomalies.shape
    mem_count = lax.axis_size("mem")
    per_dev = state_cols // BLK // mem_count
    width = per_dev * BLK
    me = lax.axis_index("mem")
    place = jnp.stack([me // 2, me % 2]).astype(jnp.int32)

    own = jnp.concatenate([obs_anomalies, innovations], axis=1)
    sent = messages(place, anomalies, width)
    up1, down1 = along_z(own, 1), along_z(own, -1)
    up2, down2 = along_z(up1, 1), along_z(down1, -1)
    up3, down3 = along_z(up2, 1), along_z(down2, -1)
    down4 = along_z(down3, -1)
    patches = [sent[0]] + [along_z(sent[j], RING[j]) for j in range(1, 8)]

    a0 = jnp.stack([own, up1, down1, up2])
    b0 = jnp.stack([down2, up3, down3, down4])
    a_up, a_down = along_reg(a0, 1), along_reg(a0, -1)
    b_up, b_down = along_reg(b0, 1), along_reg(b0, -1)
    a_up2, a_down2 = along_reg(a_up, 1), along_reg(a_down, -1)
    b_up2, b_down2 = along_reg(b_up, 1), along_reg(b_down, -1)
    windows = []
    for a, b in ((a_up2, b_up2), (a_up, b_up), (a0, b0), (a_down, b_down), (a_down2, b_down2)):
        windows += [a, b, other_core(a), other_core(b)]

    my_links = lax.dynamic_slice_in_dim(obs_links, me * per_dev, per_dev, 0)
    my_choice = lax.dynamic_slice_in_dim(taper_choice, me * per_dev, per_dev, 0)
    places = jnp.arange(20, dtype=jnp.int32)
    missed = my_links[:, :, None] != places[None, None, :]
    table = jnp.min(jnp.where(missed, 8, my_choice[:, :, None]), axis=1).reshape(-1)

    scal = jnp.concatenate([place, jnp.zeros((6,), jnp.int32), table])
    result = analyse(scal, tapers, patches, windows).reshape(mem_count, mem_dev, width)
    returned = lax.all_to_all(result, "mem", split_axis=0, concat_axis=0, tiled=True)
    return returned.transpose(1, 0, 2).reshape(mem_dev, state_cols)


def solution(mesh):
    return jax.shard_map(
        step,
        mesh=mesh,
        in_specs=(
            P("mem", "reg"),
            P("mem", "reg"),
            P("mem", "reg"),
            P("reg", None),
            P("reg", None),
            P(),
        ),
        out_specs=P("mem", "reg"),
        check_vma=False,
    )
```

profile of v0, /device:TPU:1, one launch (start us, length us, event | category | flops | bytes accessed | tf_op | source)
XLA Modules:
  0.0 211.2 jit_solution(12959327827124862073)
XLA Ops:
  1.7 6.4 %collective-permute-start.9 = (bf16[64,1024]{1,0:T(8,128)(2,1)S(1)}, bf16[64,1024]{1,0:T(8,128)(2,1)S(1)}, u32[]{:S(2)}, u32[]{:S(2)}) collective-permute-start(bf16[64,1024]{1,0:T(8,128)(2,1)S(1)} %constant_dynamic-update-slice_fusion), channel_id=1, source_target_pairs={{0,224},{16,240},{32,0},{48,16},{64,32},{80,48},{96,64},{112,80},{... | collective-permute-start | bytes 393224 | tf_op jit(solution)/shard_map/ppermute | solution.py:15
  8.1 2.2 %collective-permute-done.9 = bf16[64,1024]{1,0:T(8,128)(2,1)S(1)} collective-permute-done((bf16[64,1024]{1,0:T(8,128)(2,1)S(1)}, bf16[64,1024]{1,0:T(8,128)(2,1)S(1)}, u32[]{:S(2)}, u32[]{:S(2)}) %collective-permute-start.9) | collective-permute-done | bytes 131104 | tf_op jit(solution)/shard_map/ppermute | solution.py:15
  10.3 3.4 %collective-permute-start.13 = (bf16[64,1024]{1,0:T(8,128)(2,1)S(1)}, bf16[64,1024]{1,0:T(8,128)(2,1)S(1)}, u32[]{:S(2)}, u32[]{:S(2)}) collective-permute-start(bf16[64,1024]{1,0:T(8,128)(2,1)S(1)} %collective-permute-done.9), channel_id=1, source_target_pairs={{0,224},{16,240},{32,0},{48,16},{64,32},{80,48},{96,64},{112,80},{... | collective-permute-start | bytes 393224 | tf_op jit(solution)/shard_map/ppermute | solution.py:15
  13.7 1.9 collective-permute-done.13
  15.6 3.1 %collective-permute-start.15 = (bf16[64,1024]{1,0:T(8,128)(2,1)S(1)}, bf16[64,1024]{1,0:T(8,128)(2,1)S(1)}, u32[]{:S(2)}, u32[]{:S(2)}) collective-permute-start(bf16[64,1024]{1,0:T(8,128)(2,1)S(1)} %collective-permute-done.13), channel_id=1, source_target_pairs={{0,224},{16,240},{32,0},{48,16},{64,32},{80,48},{96,64},{112,80},{... | collective-permute-start | bytes 393224 | tf_op jit(solution)/shard_map/ppermute | solution.py:15
  18.8 5.0 %collective-permute-start.25 = (bf16[4,64,1024]{2,1,0:T(8,128)(2,1)S(1)}, bf16[4,64,1024]{2,1,0:T(8,128)(2,1)S(1)}, u32[]{:S(2)}, u32[]{:S(2)}) collective-permute-start(bf16[4,64,1024]{2,1,0:T(8,128)(2,1)S(1)} %pad_maximum_fusion.refs_16_), channel_id=1, source_target_pairs={{0,15},{1,0},{2,1},{3,2},{4,3},{5,4},{6,5},{7,6},{8,7},{9,8},{10,9... | collective-permute-start | bytes 1572872 | tf_op jit(solution)/shard_map/ppermute | solution.py:25
  23.9 1.6 copy-done
  26.3 3.3 %collective-permute-start = (bf16[8,64,1024]{2,1,0:T(8,128)(2,1)S(1)}, bf16[8,64,1024]{2,1,0:T(8,128)(2,1)S(1)}, u32[]{:S(2)}, u32[]{:S(2)}) collective-permute-start(bf16[8,64,1024]{2,1,0:T(8,128)(2,1)S(1)} %gather_other.1), channel_id=1, source_target_pairs={{0,16},{16,0},{32,48},{48,32},{64,80},{80,64},{96,112},{112,96},{1... | collective-permute-start | bytes 3145736 | tf_op jit(solution)/shard_map/ppermute | solution.py:20
  29.6 2.7 %collective-permute-start.16 = (bf16[64,1024]{1,0:T(8,128)(2,1)S(1)}, bf16[64,1024]{1,0:T(8,128)(2,1)S(1)}, u32[]{:S(2)}, u32[]{:S(2)}) collective-permute-start(bf16[64,1024]{1,0:T(8,128)(2,1)S(1)} %collective-permute-done.15), channel_id=1, source_target_pairs={{0,224},{16,240},{32,0},{48,16},{64,32},{80,48},{96,64},{112,80},{... | collective-permute-start | bytes 393224 | tf_op jit(solution)/shard_map/ppermute | solution.py:15
  32.9 2.8 %collective-permute-done.14 = bf16[64,1024]{1,0:T(8,128)(2,1)S(1)} collective-permute-done((bf16[64,1024]{1,0:T(8,128)(2,1)S(1)}, bf16[64,1024]{1,0:T(8,128)(2,1)S(1)}, u32[]{:S(2)}, u32[]{:S(2)}) %collective-permute-start.14) | collective-permute-done | bytes 131104 | tf_op jit(solution)/shard_map/ppermute | solution.py:15
  35.9 4.8 %collective-permute-start.26 = (bf16[4,64,1024]{2,1,0:T(8,128)(2,1)S(1)}, bf16[4,64,1024]{2,1,0:T(8,128)(2,1)S(1)}, u32[]{:S(2)}, u32[]{:S(2)}) collective-permute-start(bf16[4,64,1024]{2,1,0:T(8,128)(2,1)S(1)} %pad_maximum_fusion.1.refs_17_), channel_id=1, source_target_pairs={{0,15},{1,0},{2,1},{3,2},{4,3},{5,4},{6,5},{7,6},{8,7},{9,8},{10,9... | collective-permute-start | bytes 1572872 | tf_op jit(solution)/shard_map/ppermute | solution.py:25
  40.8 1.5 collective-permute-start.24
  42.3 9.4 %collective-permute-done.11.refs_12_ = bf16[4,64,1024]{2,1,0:T(8,128)(2,1)S(1)} collective-permute-done((bf16[4,64,1024]{2,1,0:T(8,128)(2,1)S(1)}, bf16[4,64,1024]{2,1,0:T(8,128)(2,1)S(1)}, u32[]{:S(2)}, u32[]{:S(2)}) %collective-permute-start.11) | collective-permute-done | bytes 524320 | tf_op jit(solution)/shard_map/ppermute | solution.py:25
  51.7 3.3 %collective-permute-start.27 = (bf16[4,64,1024]{2,1,0:T(8,128)(2,1)S(1)}, bf16[4,64,1024]{2,1,0:T(8,128)(2,1)S(1)}, u32[]{:S(2)}, u32[]{:S(2)}) collective-permute-start(bf16[4,64,1024]{2,1,0:T(8,128)(2,1)S(1)} %collective-permute-done.25.refs_20_), channel_id=1, source_target_pairs={{0,16},{16,0},{32,48},{48,32},{64,80},{80,64},{96,112},{112,96},{1... | collective-permute-start | bytes 1572872 | tf_op jit(solution)/shard_map/ppermute | solution.py:20
  55.3 1.6 collective-permute-start.12
  57.8 5.2 %collective-permute-done.17.refs_13_ = bf16[4,64,1024]{2,1,0:T(8,128)(2,1)} collective-permute-done((bf16[4,64,1024]{2,1,0:T(8,128)(2,1)S(1)}, bf16[4,64,1024]{2,1,0:T(8,128)(2,1)}, u32[]{:S(2)}, u32[]{:S(2)}) %collective-permute-start.17) | collective-permute-done | bytes 524320 | tf_op jit(solution)/shard_map/ppermute | solution.py:25
  63.0 2.7 %collective-permute-start.2 = (bf16[2,64,1024]{2,1,0:T(8,128)(2,1)S(1)}, bf16[2,64,1024]{2,1,0:T(8,128)(2,1)S(1)}, u32[]{:S(2)}, u32[]{:S(2)}) collective-permute-start(bf16[2,64,1024]{2,1,0:T(8,128)(2,1)S(1)} %get-tuple-element.15), channel_id=1, source_target_pairs={{0,224},{16,240},{32,0},{48,16},{64,32},{80,48},{96,64},{112,80},{... | collective-permute-start | bytes 786440 | tf_op jit(solution)/shard_map/ppermute | solution.py:15
  67.3 3.6 %collective-permute-start.4 = (bf16[2,64,1024]{2,1,0:T(8,128)(2,1)S(1)}, bf16[2,64,1024]{2,1,0:T(8,128)(2,1)S(1)}, u32[]{:S(2)}, u32[]{:S(2)}) collective-permute-start(bf16[2,64,1024]{2,1,0:T(8,128)(2,1)S(1)} %get-tuple-element.17), channel_id=1, source_target_pairs={{0,192},{16,208},{32,224},{48,240},{64,0},{80,16},{96,32},{112,48}... | collective-permute-start | bytes 786440 | tf_op jit(solution)/shard_map/ppermute | solution.py:15
  70.8 3.4 %collective-permute-done.12.refs_8_ = bf16[4,64,1024]{2,1,0:T(8,128)(2,1)} collective-permute-done((bf16[4,64,1024]{2,1,0:T(8,128)(2,1)S(1)}, bf16[4,64,1024]{2,1,0:T(8,128)(2,1)}, u32[]{:S(2)}, u32[]{:S(2)}) %collective-permute-start.12) | collective-permute-done | bytes 524320 | tf_op jit(solution)/shard_map/ppermute | solution.py:25
  75.7 4.7 %collective-permute-start.28 = (bf16[4,64,1024]{2,1,0:T(8,128)(2,1)S(1)}, bf16[4,64,1024]{2,1,0:T(8,128)(2,1)S(1)}, u32[]{:S(2)}, u32[]{:S(2)}) collective-permute-start(bf16[4,64,1024]{2,1,0:T(8,128)(2,1)S(1)} %collective-permute-done.26.refs_21_), channel_id=1, source_target_pairs={{0,16},{16,0},{32,48},{48,32},{64,80},{80,64},{96,112},{112,96},{1... | collective-permute-start | bytes 1572872 | tf_op jit(solution)/shard_map/ppermute | solution.py:20
  80.4 4.3 %collective-permute-done.3.refs_3_ = bf16[2,64,1024]{2,1,0:T(8,128)(2,1)S(1)} collective-permute-done((bf16[2,64,1024]{2,1,0:T(8,128)(2,1)S(1)}, bf16[2,64,1024]{2,1,0:T(8,128)(2,1)S(1)}, u32[]{:S(2)}, u32[]{:S(2)}) %collective-permute-start.3) | collective-permute-done | bytes 262176 | tf_op jit(solution)/shard_map/ppermute | solution.py:15
  86.2 5.9 %collective-permute-done.5.refs_5_ = bf16[2,64,1024]{2,1,0:T(8,128)(2,1)S(1)} collective-permute-done((bf16[2,64,1024]{2,1,0:T(8,128)(2,1)S(1)}, bf16[2,64,1024]{2,1,0:T(8,128)(2,1)S(1)}, u32[]{:S(2)}, u32[]{:S(2)}) %collective-permute-start.5) | collective-permute-done | bytes 262176 | tf_op jit(solution)/shard_map/ppermute | solution.py:15
  92.8 6.1 %collective-permute-start.7 = (bf16[2,64,1024]{2,1,0:T(8,128)(2,1)S(1)}, bf16[2,64,1024]{2,1,0:T(8,128)(2,1)S(1)}, u32[]{:S(2)}, u32[]{:S(2)}) collective-permute-start(bf16[2,64,1024]{2,1,0:T(8,128)(2,1)S(1)} %get-tuple-element.20), channel_id=1, source_target_pairs={{0,128},{16,144},{32,160},{48,176},{64,192},{80,208},{96,224},{112... | collective-permute-start | bytes 786440 | tf_op jit(solution)/shard_map/ppermute | solution.py:15
  99.6 10.2 %collective-permute-start.22 = (bf16[4,64,1024]{2,1,0:T(8,128)(2,1)}, bf16[4,64,1024]{2,1,0:T(8,128)(2,1)}, u32[]{:S(2)}, u32[]{:S(2)}) collective-permute-start(bf16[4,64,1024]{2,1,0:T(8,128)(2,1)} %collective-permute-done.17.refs_13_), channel_id=1, source_target_pairs={{0,16},{16,0},{32,48},{48,32},{64,80},{80,64},{96,112},{112,96},{1... | collective-permute-start | bytes 1572872 | tf_op jit(solution)/shard_map/ppermute | solution.py:20
  115.0 1.0 copy-done.4
  116.1 1.0 copy-done.6
  117.1 1.0 copy-done.8
  118.2 1.0 copy-done.10
  119.2 1.0 copy-done.12
  126.9 17.8 %analyse.1 = bf16[8,2,64,1024]{3,2,1,0:T(8,128)(2,1)S(1)} custom-call(s32[168]{0:T(256)S(1)} %pad_add_fusion.scal, f32[8,128,128]{2,1,0:T(8,128)S(1)} %copy-done.2, bf16[2,64,1024]{2,1,0:T(8,128)(2,1)S(1)} %get-tuple-element.13.refs_0_, bf16[2,64,1024]{2,1,0:T(8,128)(2,1)S(1)} %copy-done.14, bf16[2,64,1024]{2,1,0:T(8,128)(2,1)S(1)} %copy-done.16, ...), custom_call_target="tpu_custom_call" | custom-call | flops 11000000512 | bytes 15728640 | tf_op jit(solution)/shard_map/analyse/pallas_call | solution.py:167
  144.7 65.1 %all_to_all.5 = bf16[16,64,1024]{2,1,0:T(8,128)(2,1)S(1)} all-to-all(bf16[16,64,1024]{2,1,0:T(8,128)(2,1)S(1)} %bitcast.14), channel_id=1, replica_groups=mesh['mem'=16,'reg'=16] {'mem'}, dimensions={0} | all-to-all | bytes 4194304 | tf_op jit(solution)/shard_map/all_to_all | solution.py:223
  209.8 1.5 copy.11
  (107 shorter events, 22.4 us)
Async XLA Ops:
  1.7 8.6 %collective-permute-start.9 = (bf16[64,1024]{1,0:T(8,128)(2,1)S(1)}, bf16[64,1024]{1,0:T(8,128)(2,1)S(1)}, u32[]{:S(2)}, u32[]{:S(2)}) collective-permute-start(bf16[64,1024]{1,0:T(8,128)(2,1)S(1)} %constant_dynamic-update-slice_fusion), channel_id=1, source_target_pairs={{0,224},{16,240},{32,0},{48,16},{64,32},{80,48},{96,64},{112,80},{... | collective-permute-start | bytes 393224 | tf_op jit(solution)/shard_map/ppermute | solution.py:15
  8.1 5.6 %collective-permute-start.8 = (bf16[64,1024]{1,0:T(8,128)(2,1)S(1)}, bf16[64,1024]{1,0:T(8,128)(2,1)S(1)}, u32[]{:S(2)}, u32[]{:S(2)}) collective-permute-start(bf16[64,1024]{1,0:T(8,128)(2,1)S(1)} %constant_dynamic-update-slice_fusion), channel_id=1, source_target_pairs={{0,32},{16,48},{32,64},{48,80},{64,96},{80,112},{96,128},{112,144}... | collective-permute-start | bytes 393224 | tf_op jit(solution)/shard_map/ppermute | solution.py:15
  10.3 5.4 %collective-permute-start.13 = (bf16[64,1024]{1,0:T(8,128)(2,1)S(1)}, bf16[64,1024]{1,0:T(8,128)(2,1)S(1)}, u32[]{:S(2)}, u32[]{:S(2)}) collective-permute-start(bf16[64,1024]{1,0:T(8,128)(2,1)S(1)} %collective-permute-done.9), channel_id=1, source_target_pairs={{0,224},{16,240},{32,0},{48,16},{64,32},{80,48},{96,64},{112,80},{... | collective-permute-start | bytes 393224 | tf_op jit(solution)/shard_map/ppermute | solution.py:15
  13.7 5.0 %collective-permute-start.10 = (bf16[64,1024]{1,0:T(8,128)(2,1)S(1)}, bf16[64,1024]{1,0:T(8,128)(2,1)S(1)}, u32[]{:S(2)}, u32[]{:S(2)}) collective-permute-start(bf16[64,1024]{1,0:T(8,128)(2,1)S(1)} %collective-permute-done.8), channel_id=1, source_target_pairs={{0,32},{16,48},{32,64},{48,80},{64,96},{80,112},{96,128},{112,144}... | collective-permute-start | bytes 393224 | tf_op jit(solution)/shard_map/ppermute | solution.py:15
  15.6 14.0 %collective-permute-start.15 = (bf16[64,1024]{1,0:T(8,128)(2,1)S(1)}, bf16[64,1024]{1,0:T(8,128)(2,1)S(1)}, u32[]{:S(2)}, u32[]{:S(2)}) collective-permute-start(bf16[64,1024]{1,0:T(8,128)(2,1)S(1)} %collective-permute-done.13), channel_id=1, source_target_pairs={{0,224},{16,240},{32,0},{48,16},{64,32},{80,48},{96,64},{112,80},{... | collective-permute-start | bytes 393224 | tf_op jit(solution)/shard_map/ppermute | solution.py:15
  18.8 22.0 %collective-permute-start.25 = (bf16[4,64,1024]{2,1,0:T(8,128)(2,1)S(1)}, bf16[4,64,1024]{2,1,0:T(8,128)(2,1)S(1)}, u32[]{:S(2)}, u32[]{:S(2)}) collective-permute-start(bf16[4,64,1024]{2,1,0:T(8,128)(2,1)S(1)} %pad_maximum_fusion.refs_16_), channel_id=1, source_target_pairs={{0,15},{1,0},{2,1},{3,2},{4,3},{5,4},{6,5},{7,6},{8,7},{9,8},{10,9... | collective-permute-start | bytes 1572872 | tf_op jit(solution)/shard_map/ppermute | solution.py:25
  26.3 29.0 %collective-permute-start = (bf16[8,64,1024]{2,1,0:T(8,128)(2,1)S(1)}, bf16[8,64,1024]{2,1,0:T(8,128)(2,1)S(1)}, u32[]{:S(2)}, u32[]{:S(2)}) collective-permute-start(bf16[8,64,1024]{2,1,0:T(8,128)(2,1)S(1)} %gather_other.1), channel_id=1, source_target_pairs={{0,16},{16,0},{32,48},{48,32},{64,80},{80,64},{96,112},{112,96},{1... | collective-permute-start | bytes 3145736 | tf_op jit(solution)/shard_map/ppermute | solution.py:20
  29.6 6.2 %collective-permute-start.14 = (bf16[64,1024]{1,0:T(8,128)(2,1)S(1)}, bf16[64,1024]{1,0:T(8,128)(2,1)S(1)}, u32[]{:S(2)}, u32[]{:S(2)}) collective-permute-start(bf16[64,1024]{1,0:T(8,128)(2,1)S(1)} %collective-permute-done.10), channel_id=1, source_target_pairs={{0,32},{16,48},{32,64},{48,80},{64,96},{80,112},{96,128},{112,144}... | collective-permute-start | bytes 393224 | tf_op jit(solution)/shard_map/ppermute | solution.py:15
  29.6 6.2 %collective-permute-start.16 = (bf16[64,1024]{1,0:T(8,128)(2,1)S(1)}, bf16[64,1024]{1,0:T(8,128)(2,1)S(1)}, u32[]{:S(2)}, u32[]{:S(2)}) collective-permute-start(bf16[64,1024]{1,0:T(8,128)(2,1)S(1)} %collective-permute-done.15), channel_id=1, source_target_pairs={{0,224},{16,240},{32,0},{48,16},{64,32},{80,48},{96,64},{112,80},{... | collective-permute-start | bytes 393224 | tf_op jit(solution)/shard_map/ppermute | solution.py:15
  32.3 10.0 %collective-permute-start.23 = (bf16[4,64,1024]{2,1,0:T(8,128)(2,1)S(1)}, bf16[4,64,1024]{2,1,0:T(8,128)(2,1)S(1)}, u32[]{:S(2)}, u32[]{:S(2)}) collective-permute-start(bf16[4,64,1024]{2,1,0:T(8,128)(2,1)S(1)} %pad_maximum_fusion.refs_16_), channel_id=1, source_target_pairs={{0,16},{16,0},{32,48},{48,32},{64,80},{80,64},{96,112},{112,96},{1... | collective-permute-start | bytes 1572872 | tf_op jit(solution)/shard_map/ppermute | solution.py:20
  35.8 15.9 %collective-permute-start.11 = (bf16[4,64,1024]{2,1,0:T(8,128)(2,1)S(1)}, bf16[4,64,1024]{2,1,0:T(8,128)(2,1)S(1)}, u32[]{:S(2)}, u32[]{:S(2)}) collective-permute-start(bf16[4,64,1024]{2,1,0:T(8,128)(2,1)S(1)} %pad_maximum_fusion.refs_16_), channel_id=1, source_target_pairs={{0,1},{1,2},{2,3},{3,4},{4,5},{5,6},{6,7},{7,8},{8,9},{9,10},{10,1... | collective-permute-start | bytes 1572872 | tf_op jit(solution)/shard_map/ppermute | solution.py:25
  35.9 15.7 %collective-permute-start.26 = (bf16[4,64,1024]{2,1,0:T(8,128)(2,1)S(1)}, bf16[4,64,1024]{2,1,0:T(8,128)(2,1)S(1)}, u32[]{:S(2)}, u32[]{:S(2)}) collective-permute-start(bf16[4,64,1024]{2,1,0:T(8,128)(2,1)S(1)} %pad_maximum_fusion.1.refs_17_), channel_id=1, source_target_pairs={{0,15},{1,0},{2,1},{3,2},{4,3},{5,4},{6,5},{7,6},{8,7},{9,8},{10,9... | collective-permute-start | bytes 1572872 | tf_op jit(solution)/shard_map/ppermute | solution.py:25
  40.8 14.2 %collective-permute-start.24 = (bf16[4,64,1024]{2,1,0:T(8,128)(2,1)S(1)}, bf16[4,64,1024]{2,1,0:T(8,128)(2,1)S(1)}, u32[]{:S(2)}, u32[]{:S(2)}) collective-permute-start(bf16[4,64,1024]{2,1,0:T(8,128)(2,1)S(1)} %pad_maximum_fusion.1.refs_17_), channel_id=1, source_target_pairs={{0,16},{16,0},{32,48},{48,32},{64,80},{80,64},{96,112},{112,96},{1... | collective-permute-start | bytes 1572872 | tf_op jit(solution)/shard_map/ppermute | solution.py:20
  42.3 20.7 %collective-permute-start.17 = (bf16[4,64,1024]{2,1,0:T(8,128)(2,1)S(1)}, bf16[4,64,1024]{2,1,0:T(8,128)(2,1)}, u32[]{:S(2)}, u32[]{:S(2)}) collective-permute-start(bf16[4,64,1024]{2,1,0:T(8,128)(2,1)S(1)} %pad_maximum_fusion.1.refs_17_), channel_id=1, source_target_pairs={{0,1},{1,2},{2,3},{3,4},{4,5},{5,6},{6,7},{7,8},{8,9},{9,10},{10,1... | collective-permute-start | bytes 1572872 | tf_op jit(solution)/shard_map/ppermute | solution.py:25
  51.6 11.3 %collective-permute-start.29 = (bf16[4,64,1024]{2,1,0:T(8,128)(2,1)S(1)}, bf16[4,64,1024]{2,1,0:T(8,128)(2,1)}, u32[]{:S(2)}, u32[]{:S(2)}) collective-permute-start(bf16[4,64,1024]{2,1,0:T(8,128)(2,1)S(1)} %collective-permute-done.25.refs_20_), channel_id=1, source_target_pairs={{0,15},{1,0},{2,1},{3,2},{4,3},{5,4},{6,5},{7,6},{8,7},{9,8},{10,9... | collective-permute-start | bytes 1572872 | tf_op jit(solution)/shard_map/ppermute | solution.py:25
  51.7 14.0 %collective-permute-start.27 = (bf16[4,64,1024]{2,1,0:T(8,128)(2,1)S(1)}, bf16[4,64,1024]{2,1,0:T(8,128)(2,1)S(1)}, u32[]{:S(2)}, u32[]{:S(2)}) collective-permute-start(bf16[4,64,1024]{2,1,0:T(8,128)(2,1)S(1)} %collective-permute-done.25.refs_20_), channel_id=1, source_target_pairs={{0,16},{16,0},{32,48},{48,32},{64,80},{80,64},{96,112},{112,96},{1... | collective-permute-start | bytes 1572872 | tf_op jit(solution)/shard_map/ppermute | solution.py:20
  55.0 11.5 %collective-permute-start.21 = (bf16[4,64,1024]{2,1,0:T(8,128)(2,1)S(1)}, bf16[4,64,1024]{2,1,0:T(8,128)(2,1)S(1)}, u32[]{:S(2)}, u32[]{:S(2)}) collective-permute-start(bf16[4,64,1024]{2,1,0:T(8,128)(2,1)S(1)} %collective-permute-done.11.refs_12_), channel_id=1, source_target_pairs={{0,16},{16,0},{32,48},{48,32},{64,80},{80,64},{96,112},{112,96},{1... | collective-permute-start | bytes 1572872 | tf_op jit(solution)/shard_map/ppermute | solution.py:20
  55.3 19.0 %collective-permute-start.12 = (bf16[4,64,1024]{2,1,0:T(8,128)(2,1)S(1)}, bf16[4,64,1024]{2,1,0:T(8,128)(2,1)}, u32[]{:S(2)}, u32[]{:S(2)}) collective-permute-start(bf16[4,64,1024]{2,1,0:T(8,128)(2,1)S(1)} %collective-permute-done.11.refs_12_), channel_id=1, source_target_pairs={{0,1},{1,2},{2,3},{3,4},{4,5},{5,6},{6,7},{7,8},{8,9},{9,10},{10,1... | collective-permute-start | bytes 1572872 | tf_op jit(solution)/shard_map/ppermute | solution.py:25
  63.0 11.2 %collective-permute-start.1 = (bf16[2,64,1024]{2,1,0:T(8,128)(2,1)S(1)}, bf16[2,64,1024]{2,1,0:T(8,128)(2,1)S(1)}, u32[]{:S(2)}, u32[]{:S(2)}) collective-permute-start(bf16[2,64,1024]{2,1,0:T(8,128)(2,1)S(1)} %get-tuple-element.14), channel_id=1, source_target_pairs={{0,32},{16,48},{32,64},{48,80},{64,96},{80,112},{96,128},{112,144}... | collective-permute-start | bytes 786440 | tf_op jit(solution)/shard_map/ppermute | solution.py:15
  63.0 12.0 %collective-permute-start.2 = (bf16[2,64,1024]{2,1,0:T(8,128)(2,1)S(1)}, bf16[2,64,1024]{2,1,0:T(8,128)(2,1)S(1)}, u32[]{:S(2)}, u32[]{:S(2)}) collective-permute-start(bf16[2,64,1024]{2,1,0:T(8,128)(2,1)S(1)} %get-tuple-element.15), channel_id=1, source_target_pairs={{0,224},{16,240},{32,0},{48,16},{64,32},{80,48},{96,64},{112,80},{... | collective-permute-start | bytes 786440 | tf_op jit(solution)/shard_map/ppermute | solution.py:15
  66.5 18.3 %collective-permute-start.3 = (bf16[2,64,1024]{2,1,0:T(8,128)(2,1)S(1)}, bf16[2,64,1024]{2,1,0:T(8,128)(2,1)S(1)}, u32[]{:S(2)}, u32[]{:S(2)}) collective-permute-start(bf16[2,64,1024]{2,1,0:T(8,128)(2,1)S(1)} %get-tuple-element.16), channel_id=1, source_target_pairs={{0,64},{16,80},{32,96},{48,112},{64,128},{80,144},{96,160},{112,17... | collective-permute-start | bytes 786440 | tf_op jit(solution)/shard_map/ppermute | solution.py:15
  67.3 18.2 %collective-permute-start.4 = (bf16[2,64,1024]{2,1,0:T(8,128)(2,1)S(1)}, bf16[2,64,1024]{2,1,0:T(8,128)(2,1)S(1)}, u32[]{:S(2)}, u32[]{:S(2)}) collective-permute-start(bf16[2,64,1024]{2,1,0:T(8,128)(2,1)S(1)} %get-tuple-element.17), channel_id=1, source_target_pairs={{0,192},{16,208},{32,224},{48,240},{64,0},{80,16},{96,32},{112,48}... | collective-permute-start | bytes 786440 | tf_op jit(solution)/shard_map/ppermute | solution.py:15
  74.2 17.9 %collective-permute-start.5 = (bf16[2,64,1024]{2,1,0:T(8,128)(2,1)S(1)}, bf16[2,64,1024]{2,1,0:T(8,128)(2,1)S(1)}, u32[]{:S(2)}, u32[]{:S(2)}) collective-permute-start(bf16[2,64,1024]{2,1,0:T(8,128)(2,1)S(1)} %get-tuple-element.18), channel_id=1, source_target_pairs={{0,96},{16,112},{32,128},{48,144},{64,160},{80,176},{96,192},{112,... | collective-permute-start | bytes 786440 | tf_op jit(solution)/shard_map/ppermute | solution.py:15
  74.9 35.6 %collective-permute-start.30 = (bf16[4,64,1024]{2,1,0:T(8,128)(2,1)S(1)}, bf16[4,64,1024]{2,1,0:T(8,128)(2,1)}, u32[]{:S(2)}, u32[]{:S(2)}) collective-permute-start(bf16[4,64,1024]{2,1,0:T(8,128)(2,1)S(1)} %collective-permute-done.26.refs_21_), channel_id=1, source_target_pairs={{0,15},{1,0},{2,1},{3,2},{4,3},{5,4},{6,5},{7,6},{8,7},{9,8},{10,9... | collective-permute-start | bytes 1572872 | tf_op jit(solution)/shard_map/ppermute | solution.py:25
  75.7 35.4 %collective-permute-start.28 = (bf16[4,64,1024]{2,1,0:T(8,128)(2,1)S(1)}, bf16[4,64,1024]{2,1,0:T(8,128)(2,1)S(1)}, u32[]{:S(2)}, u32[]{:S(2)}) collective-permute-start(bf16[4,64,1024]{2,1,0:T(8,128)(2,1)S(1)} %collective-permute-done.26.refs_21_), channel_id=1, source_target_pairs={{0,16},{16,0},{32,48},{48,32},{64,80},{80,64},{96,112},{112,96},{1... | collective-permute-start | bytes 1572872 | tf_op jit(solution)/shard_map/ppermute | solution.py:20
  85.5 26.4 %collective-permute-start.18 = (bf16[4,64,1024]{2,1,0:T(8,128)(2,1)}, bf16[4,64,1024]{2,1,0:T(8,128)(2,1)}, u32[]{:S(2)}, u32[]{:S(2)}) collective-permute-start(bf16[4,64,1024]{2,1,0:T(8,128)(2,1)} %collective-permute-done.17.refs_13_), channel_id=1, source_target_pairs={{0,1},{1,2},{2,3},{3,4},{4,5},{5,6},{6,7},{7,8},{8,9},{9,10},{10,1... | collective-permute-start | bytes 1572872 | tf_op jit(solution)/shard_map/ppermute | solution.py:25
  86.2 12.7 %collective-permute-start.6 = (bf16[2,64,1024]{2,1,0:T(8,128)(2,1)S(1)}, bf16[2,64,1024]{2,1,0:T(8,128)(2,1)S(1)}, u32[]{:S(2)}, u32[]{:S(2)}) collective-permute-start(bf16[2,64,1024]{2,1,0:T(8,128)(2,1)S(1)} %get-tuple-element.19), channel_id=1, source_target_pairs={{0,160},{16,176},{32,192},{48,208},{64,224},{80,240},{96,0},{112,1... | collective-permute-start | bytes 786440 | tf_op jit(solution)/shard_map/ppermute | solution.py:15
  92.8 17.0 %collective-permute-start.7 = (bf16[2,64,1024]{2,1,0:T(8,128)(2,1)S(1)}, bf16[2,64,1024]{2,1,0:T(8,128)(2,1)S(1)}, u32[]{:S(2)}, u32[]{:S(2)}) collective-permute-start(bf16[2,64,1024]{2,1,0:T(8,128)(2,1)S(1)} %get-tuple-element.20), channel_id=1, source_target_pairs={{0,128},{16,144},{32,160},{48,176},{64,192},{80,208},{96,224},{112... | collective-permute-start | bytes 786440 | tf_op jit(solution)/shard_map/ppermute | solution.py:15
  99.6 13.1 %collective-permute-start.22 = (bf16[4,64,1024]{2,1,0:T(8,128)(2,1)}, bf16[4,64,1024]{2,1,0:T(8,128)(2,1)}, u32[]{:S(2)}, u32[]{:S(2)}) collective-permute-start(bf16[4,64,1024]{2,1,0:T(8,128)(2,1)} %collective-permute-done.17.refs_13_), channel_id=1, source_target_pairs={{0,16},{16,0},{32,48},{48,32},{64,80},{80,64},{96,112},{112,96},{1... | collective-permute-start | bytes 1572872 | tf_op jit(solution)/shard_map/ppermute | solution.py:20
  110.5 3.0 %collective-permute-start.19 = (bf16[4,64,1024]{2,1,0:T(8,128)(2,1)}, bf16[4,64,1024]{2,1,0:T(8,128)(2,1)}, u32[]{:S(2)}, u32[]{:S(2)}) collective-permute-start(bf16[4,64,1024]{2,1,0:T(8,128)(2,1)} %collective-permute-done.12.refs_8_), channel_id=1, source_target_pairs={{0,16},{16,0},{32,48},{48,32},{64,80},{80,64},{96,112},{112,96},{1... | collective-permute-start | bytes 1572872 | tf_op jit(solution)/shard_map/ppermute | solution.py:20
  111.8 2.4 %collective-permute-start.32 = (bf16[4,64,1024]{2,1,0:T(8,128)(2,1)}, bf16[4,64,1024]{2,1,0:T(8,128)(2,1)}, u32[]{:S(2)}, u32[]{:S(2)}) collective-permute-start(bf16[4,64,1024]{2,1,0:T(8,128)(2,1)} %collective-permute-done.30.refs_25_), channel_id=1, source_target_pairs={{0,16},{16,0},{32,48},{48,32},{64,80},{80,64},{96,112},{112,96},{1... | collective-permute-start | bytes 1572872 | tf_op jit(solution)/shard_map/ppermute | solution.py:20
  111.9 3.2 %collective-permute-start.20 = (bf16[4,64,1024]{2,1,0:T(8,128)(2,1)}, bf16[4,64,1024]{2,1,0:T(8,128)(2,1)}, u32[]{:S(2)}, u32[]{:S(2)}) collective-permute-start(bf16[4,64,1024]{2,1,0:T(8,128)(2,1)} %collective-permute-done.18.refs_9_), channel_id=1, source_target_pairs={{0,16},{16,0},{32,48},{48,32},{64,80},{80,64},{96,112},{112,96},{1... | collective-permute-start | bytes 1572872 | tf_op jit(solution)/shard_map/ppermute | solution.py:20
  (30 other events, 366.3 us)
where the time goes:
time: 212 us; the launch traced here: 211 us
  blocking collectives  65.1 us (31%)
  starting transfers between devices  64.5 us (30%)
  waiting for transfers between devices  37.5 us (18%)
  local copies, waits for them, and re-layouts  24.2 us (11%)
  Pallas kernels  19.5 us (9%)
    all_to_all x1, blocking collectives, step(): lax.all_to_all(result, 'mem', split_axis=0, concat_axis=0, tiled=True)  65.1 us
    ppermute x14, starting transfers between devices, along_z(): lax.ppermute(x, 'mem', [(i, (i + 2 * by) % size) for i in range(size)])  27.9 us
    ppermute x11, starting transfers between devices, other_core(): return lax.ppermute(x, 'mem', [(i, i ^ 1) for i in range(size)])  25 us
    unnamed x59, local copies, waits for them, and re-layouts  21.7 us
    ppermute x8, waiting for transfers between devices, along_reg(): return lax.ppermute(x, 'reg', [(i, (i + by) % size) for i in range(size)])  17.9 us
    pallas_call x1, Pallas kernels, analyse(): pl.pallas_call(body, out_shape=jax.ShapeDtypeStruct((8, 2, members, width...  17.8 us
    ppermute x14, waiting for transfers between devices, along_z(): lax.ppermute(x, 'mem', [(i, (i + 2 * by) % size) for i in range(size)])  17.2 us
    ppermute x8, starting transfers between devices, along_reg(): return lax.ppermute(x, 'reg', [(i, (i + by) % size) for i in range(size)])  11.5 us
  transfers between devices with their start and end apart: 33, of which 12 were waited for; matrix products, arithmetic and copies ran while one was open for 0% of the time, Pallas kernels for 1%

commit v1 on v0

--- a/solution.py
+++ b/solution.py
@@ -1,3 +1,5 @@
+import functools
+
 import jax
 import jax.numpy as jnp
 from jax import lax
@@ -6,6 +8,7 @@
 from jax.sharding import PartitionSpec as P
 
 BLK = 128
+PARTS = 2
 
 RING = (0, 1, -1, 2, -2, 3, -3, 4)
 
@@ -84,7 +87,7 @@
     )(place, anomalies, other)
 
 
-def body(scal, tapers, *refs):
+def body(part, scal, tapers, *refs):
     patches = refs[:8]
     windows = refs[8:28]
     out, held, obs, innov, cols, tapered, scaled, done, in_sems, out_sems = refs[28:]
@@ -94,7 +97,8 @@
     slices = obs.shape[1]
     count = obs.shape[-1]
     depth = slices * 64
-    copies = [pltpu.make_async_copy(patches[j], held.at[j], in_sems.at[j]) for j in range(8)]
+    mine = pl.ds(part * width, width)
+    copies = [pltpu.make_async_copy(patches[j].at[:, :, mine], held.at[j], in_sems.at[j]) for j in range(8)]
     obs_copies = [
         pltpu.make_async_copy(windows[k].at[:, :, pl.ds(0, count)], obs.at[k], in_sems.at[8 + k]) for k in range(20)
     ]
@@ -129,7 +133,7 @@
             for b in range(width // BLK):
                 for w in range(2):
                     at = region * 512 + half * 256 + w * BLK
-                    t = scal[8 + b * 20 + at // BLK]
+                    t = scal[8 + (part * (width // BLK) + b) * 20 + at // BLK]
                     tile = cov[b * BLK : (b + 1) * BLK, w * BLK : (w + 1) * BLK] * scaled[t]
                     tapered[pl.ds(b * BLK, BLK), pl.ds(at, BLK)] = tile.astype(jnp.bfloat16)
 
@@ -158,14 +162,14 @@
         copy.wait()
 
 
-def analyse(scal, tapers, patches, windows):
+def analyse(part, scal, tapers, patches, windows):
     smem = pl.BlockSpec(memory_space=pltpu.SMEM)
     vmem = pl.BlockSpec(memory_space=pltpu.VMEM)
     hbm = pl.BlockSpec(memory_space=pltpu.HBM)
-    members, width = patches[0].shape[1:]
+    members, width = patches[0].shape[1], patches[0].shape[2] // PARTS
     slices = windows[0].shape[0]
     return pl.pallas_call(
-        body,
+        functools.partial(body, part),
         out_shape=jax.ShapeDtypeStruct((8, 2, members, width), jnp.bfloat16),
         in_specs=[smem, vmem] + [hbm] * 28,
         out_specs=hbm,
@@ -180,8 +184,8 @@
             pltpu.SemaphoreType.DMA((48,)),
             pltpu.SemaphoreType.DMA((16,)),
         ],
-        compiler_params=pltpu.CompilerParams(vmem_limit_bytes=24 << 20),
-        cost_estimate=pl.CostEstimate(flops=11 * 10**9, bytes_accessed=15 << 20, transcendentals=0),
+        compiler_params=pltpu.CompilerParams(vmem_limit_bytes=56 << 20),
+        cost_estimate=pl.CostEstimate(flops=11 * 10**9 // PARTS, bytes_accessed=15 << 20, transcendentals=0),
         name="analyse",
     )(scal, tapers, *patches, *windows)
 
@@ -219,9 +223,12 @@
     table = jnp.min(jnp.where(missed, 8, my_choice[:, :, None]), axis=1).reshape(-1)
 
     scal = jnp.concatenate([place, jnp.zeros((6,), jnp.int32), table])
-    result = analyse(scal, tapers, patches, windows).reshape(mem_count, mem_dev, width)
-    returned = lax.all_to_all(result, "mem", split_axis=0, concat_axis=0, tiled=True)
-    return returned.transpose(1, 0, 2).reshape(mem_dev, state_cols)
+    returned = []
+    for part in range(PARTS):
+        result = analyse(part, scal, tapers, patches, windows).reshape(mem_count, mem_dev, width // PARTS)
+        returned.append(lax.all_to_all(result, "mem", split_axis=0, concat_axis=0, tiled=True))
+    whole = jnp.concatenate(returned, axis=2)
+    return whole.transpose(1, 0, 2).reshape(mem_dev, state_cols)
 
 
 def solution(mesh):

time: 212 us -> 200 us (0.943)
  blocking collectives: 65.1 us -> 31.8 us
  waiting for transfers between devices: 37.5 us -> 62.8 us
  local copies, waits for them, and re-layouts: 24.2 us -> 6.47 us
  starting transfers between devices: 64.5 us -> 72.7 us
  Pallas kernels: 19.5 us -> 23.8 us
    all_to_all x1, blocking collectives: 65.1 us -> 31.8 us  [step(): lax.all_to_all(result, 'mem', split_axis=0, concat_axis=0, tiled=True)]
    unnamed x59 -> x47, local copies, waits for them, and re-layouts: 21.7 us -> 3.95 us
    all_to_all x0 -> x1, waiting for transfers between devices: none -> 17 us  [step(): lax.all_to_all(result, 'mem', split_axis=0, concat_axis=0, tiled=True)]
    all_to_all x0 -> x1, starting transfers between devices: none -> 11.9 us  [step(): lax.all_to_all(result, 'mem', split_axis=0, concat_axis=0, tiled=True)]
    ppermute x14, waiting for transfers between devices: 17.2 us -> 25.8 us  [along_z(): lax.ppermute(x, 'mem', [(i, (i + 2 * by) % size) for i in range(size)])]
    pallas_call x1 -> x2, Pallas kernels: 17.8 us -> 22.1 us  [analyse(): pl.pallas_call(functools.partial(body, part), out_shape=jax.ShapeDtypeStr...]
    ppermute x11, starting transfers between devices: 25 us -> 20.8 us  [other_core(): return lax.ppermute(x, 'mem', [(i, i ^ 1) for i in range(size)])]
  transfers between devices with their start and end apart: 33 -> 34, of which waited for: 12 -> 13; matrix products, arithmetic and copies ran while one was open for 0% -> 1% of each run, Pallas kernels for 1% -> 6%
where the time goes in v1:
time: 200 us; the launch traced here: 199 us
  starting transfers between devices  72.7 us (36%)
  waiting for transfers between devices  62.8 us (31%)
  blocking collectives  31.8 us (16%)
  Pallas kernels  23.8 us (12%)
  local copies, waits for them, and re-layouts  6.47 us (3%)
    all_to_all x1, blocking collectives, step(): lax.all_to_all(result, 'mem', split_axis=0, concat_axis=0, tiled=True)  31.8 us
    ppermute x14, starting transfers between devices, along_z(): lax.ppermute(x, 'mem', [(i, (i + 2 * by) % size) for i in range(size)])  28.4 us
    ppermute x14, waiting for transfers between devices, along_z(): lax.ppermute(x, 'mem', [(i, (i + 2 * by) % size) for i in range(size)])  25.8 us
    pallas_call x2, Pallas kernels, analyse(): pl.pallas_call(functools.partial(body, part), out_shape=jax.ShapeDtypeStr...  22.1 us
    ppermute x11, starting transfers between devices, other_core(): return lax.ppermute(x, 'mem', [(i, i ^ 1) for i in range(size)])  20.8 us
    ppermute x8, waiting for transfers between devices, along_reg(): return lax.ppermute(x, 'reg', [(i, (i + by) % size) for i in range(size)])  18.3 us
    all_to_all x1, waiting for transfers between devices, step(): lax.all_to_all(result, 'mem', split_axis=0, concat_axis=0, tiled=True)  17 us
    all_to_all x1, starting transfers between devices, step(): lax.all_to_all(result, 'mem', split_axis=0, concat_axis=0, tiled=True)  11.9 us
  transfers between devices with their start and end apart: 34, of which 13 were waited for; matrix products, arithmetic and copies ran while one was open for 1% of the time, Pallas kernels for 6%

profile of v1, /device:TPU:1, one launch (start us, length us, event | category | flops | bytes accessed | tf_op | source)
XLA Modules:
  0.0 199.1 jit_solution(11514223812270591124)
XLA Ops:
  1.7 6.4 %collective-permute-start.9 = (bf16[64,1024]{1,0:T(8,128)(2,1)S(1)}, bf16[64,1024]{1,0:T(8,128)(2,1)S(1)}, u32[]{:S(2)}, u32[]{:S(2)}) collective-permute-start(bf16[64,1024]{1,0:T(8,128)(2,1)S(1)} %constant_dynamic-update-slice_fusion), channel_id=1, source_target_pairs={{0,224},{16,240},{32,0},{48,16},{64,32},{80,48},{96,64},{112,80},{... | collective-permute-start | bytes 393224 | tf_op jit(solution)/shard_map/ppermute | solution.py:18
  8.1 2.2 %collective-permute-done.9 = bf16[64,1024]{1,0:T(8,128)(2,1)S(1)} collective-permute-done((bf16[64,1024]{1,0:T(8,128)(2,1)S(1)}, bf16[64,1024]{1,0:T(8,128)(2,1)S(1)}, u32[]{:S(2)}, u32[]{:S(2)}) %collective-permute-start.9) | collective-permute-done | bytes 131104 | tf_op jit(solution)/shard_map/ppermute | solution.py:18
  10.3 3.4 %collective-permute-start.13 = (bf16[64,1024]{1,0:T(8,128)(2,1)S(1)}, bf16[64,1024]{1,0:T(8,128)(2,1)S(1)}, u32[]{:S(2)}, u32[]{:S(2)}) collective-permute-start(bf16[64,1024]{1,0:T(8,128)(2,1)S(1)} %collective-permute-done.9), channel_id=1, source_target_pairs={{0,224},{16,240},{32,0},{48,16},{64,32},{80,48},{96,64},{112,80},{... | collective-permute-start | bytes 393224 | tf_op jit(solution)/shard_map/ppermute | solution.py:18
  13.7 1.9 collective-permute-done.13
  15.6 3.1 %collective-permute-start.15 = (bf16[64,1024]{1,0:T(8,128)(2,1)S(1)}, bf16[64,1024]{1,0:T(8,128)(2,1)S(1)}, u32[]{:S(2)}, u32[]{:S(2)}) collective-permute-start(bf16[64,1024]{1,0:T(8,128)(2,1)S(1)} %collective-permute-done.13), channel_id=1, source_target_pairs={{0,224},{16,240},{32,0},{48,16},{64,32},{80,48},{96,64},{112,80},{... | collective-permute-start | bytes 393224 | tf_op jit(solution)/shard_map/ppermute | solution.py:18
  18.8 5.0 %collective-permute-start.25 = (bf16[4,64,1024]{2,1,0:T(8,128)(2,1)S(1)}, bf16[4,64,1024]{2,1,0:T(8,128)(2,1)S(1)}, u32[]{:S(2)}, u32[]{:S(2)}) collective-permute-start(bf16[4,64,1024]{2,1,0:T(8,128)(2,1)S(1)} %pad_maximum_fusion.refs_16_), channel_id=1, source_target_pairs={{0,15},{1,0},{2,1},{3,2},{4,3},{5,4},{6,5},{7,6},{8,7},{9,8},{10,9... | collective-permute-start | bytes 1572872 | tf_op jit(solution)/shard_map/ppermute | solution.py:28
  23.9 1.6 copy-done
  26.3 3.3 %collective-permute-start = (bf16[8,64,1024]{2,1,0:T(8,128)(2,1)S(1)}, bf16[8,64,1024]{2,1,0:T(8,128)(2,1)S(1)}, u32[]{:S(2)}, u32[]{:S(2)}) collective-permute-start(bf16[8,64,1024]{2,1,0:T(8,128)(2,1)S(1)} %gather_other.1), channel_id=1, source_target_pairs={{0,16},{16,0},{32,48},{48,32},{64,80},{80,64},{96,112},{112,96},{1... | collective-permute-start | bytes 3145736 | tf_op jit(solution)/shard_map/ppermute | solution.py:23
  29.6 2.7 %collective-permute-start.16 = (bf16[64,1024]{1,0:T(8,128)(2,1)S(1)}, bf16[64,1024]{1,0:T(8,128)(2,1)S(1)}, u32[]{:S(2)}, u32[]{:S(2)}) collective-permute-start(bf16[64,1024]{1,0:T(8,128)(2,1)S(1)} %collective-permute-done.15), channel_id=1, source_target_pairs={{0,224},{16,240},{32,0},{48,16},{64,32},{80,48},{96,64},{112,80},{... | collective-permute-start | bytes 393224 | tf_op jit(solution)/shard_map/ppermute | solution.py:18
  33.0 2.8 %collective-permute-done.14 = bf16[64,1024]{1,0:T(8,128)(2,1)S(1)} collective-permute-done((bf16[64,1024]{1,0:T(8,128)(2,1)S(1)}, bf16[64,1024]{1,0:T(8,128)(2,1)S(1)}, u32[]{:S(2)}, u32[]{:S(2)}) %collective-permute-start.14) | collective-permute-done | bytes 131104 | tf_op jit(solution)/shard_map/ppermute | solution.py:18
  35.9 4.8 %collective-permute-start.26 = (bf16[4,64,1024]{2,1,0:T(8,128)(2,1)S(1)}, bf16[4,64,1024]{2,1,0:T(8,128)(2,1)S(1)}, u32[]{:S(2)}, u32[]{:S(2)}) collective-permute-start(bf16[4,64,1024]{2,1,0:T(8,128)(2,1)S(1)} %pad_maximum_fusion.1.refs_17_), channel_id=1, source_target_pairs={{0,15},{1,0},{2,1},{3,2},{4,3},{5,4},{6,5},{7,6},{8,7},{9,8},{10,9... | collective-permute-start | bytes 1572872 | tf_op jit(solution)/shard_map/ppermute | solution.py:28
  40.8 1.5 collective-permute-start.24
  42.3 9.4 %collective-permute-done.11.refs_12_ = bf16[4,64,1024]{2,1,0:T(8,128)(2,1)S(1)} collective-permute-done((bf16[4,64,1024]{2,1,0:T(8,128)(2,1)S(1)}, bf16[4,64,1024]{2,1,0:T(8,128)(2,1)S(1)}, u32[]{:S(2)}, u32[]{:S(2)}) %collective-permute-start.11) | collective-permute-done | bytes 524320 | tf_op jit(solution)/shard_map/ppermute | solution.py:28
  51.7 3.3 %collective-permute-start.27 = (bf16[4,64,1024]{2,1,0:T(8,128)(2,1)S(1)}, bf16[4,64,1024]{2,1,0:T(8,128)(2,1)S(1)}, u32[]{:S(2)}, u32[]{:S(2)}) collective-permute-start(bf16[4,64,1024]{2,1,0:T(8,128)(2,1)S(1)} %collective-permute-done.25.refs_20_), channel_id=1, source_target_pairs={{0,16},{16,0},{32,48},{48,32},{64,80},{80,64},{96,112},{112,96},{1... | collective-permute-start | bytes 1572872 | tf_op jit(solution)/shard_map/ppermute | solution.py:23
  55.8 1.6 collective-permute-start.12
  59.0 4.0 %collective-permute-done.17.refs_13_ = bf16[4,64,1024]{2,1,0:T(8,128)(2,1)} collective-permute-done((bf16[4,64,1024]{2,1,0:T(8,128)(2,1)S(1)}, bf16[4,64,1024]{2,1,0:T(8,128)(2,1)}, u32[]{:S(2)}, u32[]{:S(2)}) %collective-permute-start.17) | collective-permute-done | bytes 524320 | tf_op jit(solution)/shard_map/ppermute | solution.py:28
  63.0 2.7 %collective-permute-start.2 = (bf16[2,64,1024]{2,1,0:T(8,128)(2,1)S(1)}, bf16[2,64,1024]{2,1,0:T(8,128)(2,1)S(1)}, u32[]{:S(2)}, u32[]{:S(2)}) collective-permute-start(bf16[2,64,1024]{2,1,0:T(8,128)(2,1)S(1)} %get-tuple-element.15), channel_id=1, source_target_pairs={{0,224},{16,240},{32,0},{48,16},{64,32},{80,48},{96,64},{112,80},{... | collective-permute-start | bytes 786440 | tf_op jit(solution)/shard_map/ppermute | solution.py:18
  65.7 3.6 %collective-permute-start.4 = (bf16[2,64,1024]{2,1,0:T(8,128)(2,1)S(1)}, bf16[2,64,1024]{2,1,0:T(8,128)(2,1)S(1)}, u32[]{:S(2)}, u32[]{:S(2)}) collective-permute-start(bf16[2,64,1024]{2,1,0:T(8,128)(2,1)S(1)} %get-tuple-element.17), channel_id=1, source_target_pairs={{0,192},{16,208},{32,224},{48,240},{64,0},{80,16},{96,32},{112,48}... | collective-permute-start | bytes 786440 | tf_op jit(solution)/shard_map/ppermute | solution.py:18
  69.3 5.0 %collective-permute-done.12.refs_8_ = bf16[4,64,1024]{2,1,0:T(8,128)(2,1)} collective-permute-done((bf16[4,64,1024]{2,1,0:T(8,128)(2,1)S(1)}, bf16[4,64,1024]{2,1,0:T(8,128)(2,1)}, u32[]{:S(2)}, u32[]{:S(2)}) %collective-permute-start.12) | collective-permute-done | bytes 524320 | tf_op jit(solution)/shard_map/ppermute | solution.py:28
  74.4 5.1 %collective-permute-start.28 = (bf16[4,64,1024]{2,1,0:T(8,128)(2,1)S(1)}, bf16[4,64,1024]{2,1,0:T(8,128)(2,1)S(1)}, u32[]{:S(2)}, u32[]{:S(2)}) collective-permute-start(bf16[4,64,1024]{2,1,0:T(8,128)(2,1)S(1)} %collective-permute-done.26.refs_21_), channel_id=1, source_target_pairs={{0,16},{16,0},{32,48},{48,32},{64,80},{80,64},{96,112},{112,96},{1... | collective-permute-start | bytes 1572872 | tf_op jit(solution)/shard_map/ppermute | solution.py:23
  79.5 2.6 %collective-permute-done.3.refs_3_ = bf16[2,64,1024]{2,1,0:T(8,128)(2,1)S(1)} collective-permute-done((bf16[2,64,1024]{2,1,0:T(8,128)(2,1)S(1)}, bf16[2,64,1024]{2,1,0:T(8,128)(2,1)S(1)}, u32[]{:S(2)}, u32[]{:S(2)}) %collective-permute-start.3) | collective-permute-done | bytes 262176 | tf_op jit(solution)/shard_map/ppermute | solution.py:18
  82.6 9.1 %collective-permute-done.5.refs_5_ = bf16[2,64,1024]{2,1,0:T(8,128)(2,1)S(1)} collective-permute-done((bf16[2,64,1024]{2,1,0:T(8,128)(2,1)S(1)}, bf16[2,64,1024]{2,1,0:T(8,128)(2,1)S(1)}, u32[]{:S(2)}, u32[]{:S(2)}) %collective-permute-start.5) | collective-permute-done | bytes 262176 | tf_op jit(solution)/shard_map/ppermute | solution.py:18
  91.7 6.2 %collective-permute-start.7 = (bf16[2,64,1024]{2,1,0:T(8,128)(2,1)S(1)}, bf16[2,64,1024]{2,1,0:T(8,128)(2,1)S(1)}, u32[]{:S(2)}, u32[]{:S(2)}) collective-permute-start(bf16[2,64,1024]{2,1,0:T(8,128)(2,1)S(1)} %get-tuple-element.20), channel_id=1, source_target_pairs={{0,128},{16,144},{32,160},{48,176},{64,192},{80,208},{96,224},{112... | collective-permute-start | bytes 786440 | tf_op jit(solution)/shard_map/ppermute | solution.py:18
  97.8 3.1 %collective-permute-start.22 = (bf16[4,64,1024]{2,1,0:T(8,128)(2,1)}, bf16[4,64,1024]{2,1,0:T(8,128)(2,1)}, u32[]{:S(2)}, u32[]{:S(2)}) collective-permute-start(bf16[4,64,1024]{2,1,0:T(8,128)(2,1)} %collective-permute-done.17.refs_13_), channel_id=1, source_target_pairs={{0,16},{16,0},{32,48},{48,32},{64,80},{80,64},{96,112},{112,96},{1... | collective-permute-start | bytes 1572872 | tf_op jit(solution)/shard_map/ppermute | solution.py:23
  100.9 7.1 %collective-permute-done.7.refs_7_ = bf16[2,64,1024]{2,1,0:T(8,128)(2,1)S(1)} collective-permute-done((bf16[2,64,1024]{2,1,0:T(8,128)(2,1)S(1)}, bf16[2,64,1024]{2,1,0:T(8,128)(2,1)S(1)}, u32[]{:S(2)}, u32[]{:S(2)}) %collective-permute-start.7) | collective-permute-done | bytes 262176 | tf_op jit(solution)/shard_map/ppermute | solution.py:18
  108.1 2.5 %collective-permute-start.31 = (bf16[4,64,1024]{2,1,0:T(8,128)(2,1)S(1)}, bf16[4,64,1024]{2,1,0:T(8,128)(2,1)}, u32[]{:S(2)}, u32[]{:S(2)}) collective-permute-start(bf16[4,64,1024]{2,1,0:T(8,128)(2,1)S(1)} %collective-permute-done.29.refs_24_), channel_id=1, source_target_pairs={{0,16},{16,0},{32,48},{48,32},{64,80},{80,64},{96,112},{112,96},{1... | collective-permute-start | bytes 1572872 | tf_op jit(solution)/shard_map/ppermute | solution.py:23
  114.5 11.1 %analyse.3 = bf16[8,2,64,512]{3,2,1,0:T(8,128)(2,1)} custom-call(s32[168]{0:T(256)} %pad_add_fusion.scal, f32[8,128,128]{2,1,0:T(8,128)} %tapers.3, bf16[2,64,1024]{2,1,0:T(8,128)(2,1)} %copy-done.2, bf16[2,64,1024]{2,1,0:T(8,128)(2,1)} %copy-done.16, bf16[2,64,1024]{2,1,0:T(8,128)(2,1)} %copy-done.17, bf16[2,64,1024]{2,1,0:T(8,128)(2,1)} %copy-done.18, ...), custom_call_target="tpu_custom_call" | custom-call | flops 5500000256 | bytes 15728640 | tf_op jit(solution)/shard_map/analyse/pallas_call | solution.py:171
  125.6 11.9 %all-to-all-start.1 = ((bf16[16,64,512]{2,1,0:T(8,128)(2,1)}), bf16[16,64,512]{2,1,0:T(8,128)(2,1)S(1)}, u32[]{:S(2)}, u32[]{:S(2)}) async-start(bf16[16,64,512]{2,1,0:T(8,128)(2,1)} %bitcast.16), calls=%async_computation.1 | async-start | bytes 2097152 | tf_op jit(solution)/shard_map/all_to_all | solution.py:229
  137.5 11.0 %analyse.2 = bf16[8,2,64,512]{3,2,1,0:T(8,128)(2,1)} custom-call(s32[168]{0:T(256)} %pad_add_fusion.scal, f32[8,128,128]{2,1,0:T(8,128)} %tapers.3, bf16[2,64,1024]{2,1,0:T(8,128)(2,1)} %copy-done.2, bf16[2,64,1024]{2,1,0:T(8,128)(2,1)} %copy-done.16, bf16[2,64,1024]{2,1,0:T(8,128)(2,1)} %copy-done.17, bf16[2,64,1024]{2,1,0:T(8,128)(2,1)} %copy-done.18, ...), custom_call_target="tpu_custom_call" | custom-call | flops 5500000256 | bytes 15728640 | tf_op jit(solution)/shard_map/analyse/pallas_call | solution.py:171
  148.6 17.0 %all-to-all-done.1 = bf16[16,64,512]{2,1,0:T(8,128)(2,1)S(1)} async-done(((bf16[16,64,512]{2,1,0:T(8,128)(2,1)}), bf16[16,64,512]{2,1,0:T(8,128)(2,1)S(1)}, u32[]{:S(2)}, u32[]{:S(2)}) %all-to-all-start.1) | async-done | bytes 1048608 | tf_op jit(solution)/shard_map/all_to_all | solution.py:229
  165.5 31.8 %all_to_all.10 = bf16[16,64,512]{2,1,0:T(8,128)(2,1)S(1)} all-to-all(bf16[16,64,512]{2,1,0:T(8,128)(2,1)} %bitcast.17), channel_id=1, replica_groups=mesh['mem'=16,'reg'=16] {'mem'}, dimensions={0} | all-to-all | bytes 2097152 | tf_op jit(solution)/shard_map/all_to_all | solution.py:229
  197.6 1.5 copy.11
  (99 shorter events, 10.5 us)
Async XLA Ops:
  1.7 8.6 %collective-permute-start.9 = (bf16[64,1024]{1,0:T(8,128)(2,1)S(1)}, bf16[64,1024]{1,0:T(8,128)(2,1)S(1)}, u32[]{:S(2)}, u32[]{:S(2)}) collective-permute-start(bf16[64,1024]{1,0:T(8,128)(2,1)S(1)} %constant_dynamic-update-slice_fusion), channel_id=1, source_target_pairs={{0,224},{16,240},{32,0},{48,16},{64,32},{80,48},{96,64},{112,80},{... | collective-permute-start | bytes 393224 | tf_op jit(solution)/shard_map/ppermute | solution.py:18
  8.1 5.6 %collective-permute-start.8 = (bf16[64,1024]{1,0:T(8,128)(2,1)S(1)}, bf16[64,1024]{1,0:T(8,128)(2,1)S(1)}, u32[]{:S(2)}, u32[]{:S(2)}) collective-permute-start(bf16[64,1024]{1,0:T(8,128)(2,1)S(1)} %constant_dynamic-update-slice_fusion), channel_id=1, source_target_pairs={{0,32},{16,48},{32,64},{48,80},{64,96},{80,112},{96,128},{112,144}... | collective-permute-start | bytes 393224 | tf_op jit(solution)/shard_map/ppermute | solution.py:18
  10.3 5.4 %collective-permute-start.13 = (bf16[64,1024]{1,0:T(8,128)(2,1)S(1)}, bf16[64,1024]{1,0:T(8,128)(2,1)S(1)}, u32[]{:S(2)}, u32[]{:S(2)}) collective-permute-start(bf16[64,1024]{1,0:T(8,128)(2,1)S(1)} %collective-permute-done.9), channel_id=1, source_target_pairs={{0,224},{16,240},{32,0},{48,16},{64,32},{80,48},{96,64},{112,80},{... | collective-permute-start | bytes 393224 | tf_op jit(solution)/shard_map/ppermute | solution.py:18
  13.7 5.0 %collective-permute-start.10 = (bf16[64,1024]{1,0:T(8,128)(2,1)S(1)}, bf16[64,1024]{1,0:T(8,128)(2,1)S(1)}, u32[]{:S(2)}, u32[]{:S(2)}) collective-permute-start(bf16[64,1024]{1,0:T(8,128)(2,1)S(1)} %collective-permute-done.8), channel_id=1, source_target_pairs={{0,32},{16,48},{32,64},{48,80},{64,96},{80,112},{96,128},{112,144}... | collective-permute-start | bytes 393224 | tf_op jit(solution)/shard_map/ppermute | solution.py:18
  15.6 14.0 %collective-permute-start.15 = (bf16[64,1024]{1,0:T(8,128)(2,1)S(1)}, bf16[64,1024]{1,0:T(8,128)(2,1)S(1)}, u32[]{:S(2)}, u32[]{:S(2)}) collective-permute-start(bf16[64,1024]{1,0:T(8,128)(2,1)S(1)} %collective-permute-done.13), channel_id=1, source_target_pairs={{0,224},{16,240},{32,0},{48,16},{64,32},{80,48},{96,64},{112,80},{... | collective-permute-start | bytes 393224 | tf_op jit(solution)/shard_map/ppermute | solution.py:18
  18.8 22.0 %collective-permute-start.25 = (bf16[4,64,1024]{2,1,0:T(8,128)(2,1)S(1)}, bf16[4,64,1024]{2,1,0:T(8,128)(2,1)S(1)}, u32[]{:S(2)}, u32[]{:S(2)}) collective-permute-start(bf16[4,64,1024]{2,1,0:T(8,128)(2,1)S(1)} %pad_maximum_fusion.refs_16_), channel_id=1, source_target_pairs={{0,15},{1,0},{2,1},{3,2},{4,3},{5,4},{6,5},{7,6},{8,7},{9,8},{10,9... | collective-permute-start | bytes 1572872 | tf_op jit(solution)/shard_map/ppermute | solution.py:28
  26.3 29.0 %collective-permute-start = (bf16[8,64,1024]{2,1,0:T(8,128)(2,1)S(1)}, bf16[8,64,1024]{2,1,0:T(8,128)(2,1)S(1)}, u32[]{:S(2)}, u32[]{:S(2)}) collective-permute-start(bf16[8,64,1024]{2,1,0:T(8,128)(2,1)S(1)} %gather_other.1), channel_id=1, source_target_pairs={{0,16},{16,0},{32,48},{48,32},{64,80},{80,64},{96,112},{112,96},{1... | collective-permute-start | bytes 3145736 | tf_op jit(solution)/shard_map/ppermute | solution.py:23
  29.6 6.2 %collective-permute-start.14 = (bf16[64,1024]{1,0:T(8,128)(2,1)S(1)}, bf16[64,1024]{1,0:T(8,128)(2,1)S(1)}, u32[]{:S(2)}, u32[]{:S(2)}) collective-permute-start(bf16[64,1024]{1,0:T(8,128)(2,1)S(1)} %collective-permute-done.10), channel_id=1, source_target_pairs={{0,32},{16,48},{32,64},{48,80},{64,96},{80,112},{96,128},{112,144}... | collective-permute-start | bytes 393224 | tf_op jit(solution)/shard_map/ppermute | solution.py:18
  29.6 6.2 %collective-permute-start.16 = (bf16[64,1024]{1,0:T(8,128)(2,1)S(1)}, bf16[64,1024]{1,0:T(8,128)(2,1)S(1)}, u32[]{:S(2)}, u32[]{:S(2)}) collective-permute-start(bf16[64,1024]{1,0:T(8,128)(2,1)S(1)} %collective-permute-done.15), channel_id=1, source_target_pairs={{0,224},{16,240},{32,0},{48,16},{64,32},{80,48},{96,64},{112,80},{... | collective-permute-start | bytes 393224 | tf_op jit(solution)/shard_map/ppermute | solution.py:18
  32.3 10.0 %collective-permute-start.23 = (bf16[4,64,1024]{2,1,0:T(8,128)(2,1)S(1)}, bf16[4,64,1024]{2,1,0:T(8,128)(2,1)S(1)}, u32[]{:S(2)}, u32[]{:S(2)}) collective-permute-start(bf16[4,64,1024]{2,1,0:T(8,128)(2,1)S(1)} %pad_maximum_fusion.refs_16_), channel_id=1, source_target_pairs={{0,16},{16,0},{32,48},{48,32},{64,80},{80,64},{96,112},{112,96},{1... | collective-permute-start | bytes 1572872 | tf_op jit(solution)/shard_map/ppermute | solution.py:23
  35.8 15.9 %collective-permute-start.11 = (bf16[4,64,1024]{2,1,0:T(8,128)(2,1)S(1)}, bf16[4,64,1024]{2,1,0:T(8,128)(2,1)S(1)}, u32[]{:S(2)}, u32[]{:S(2)}) collective-permute-start(bf16[4,64,1024]{2,1,0:T(8,128)(2,1)S(1)} %pad_maximum_fusion.refs_16_), channel_id=1, source_target_pairs={{0,1},{1,2},{2,3},{3,4},{4,5},{5,6},{6,7},{7,8},{8,9},{9,10},{10,1... | collective-permute-start | bytes 1572872 | tf_op jit(solution)/shard_map/ppermute | solution.py:28
  35.9 15.7 %collective-permute-start.26 = (bf16[4,64,1024]{2,1,0:T(8,128)(2,1)S(1)}, bf16[4,64,1024]{2,1,0:T(8,128)(2,1)S(1)}, u32[]{:S(2)}, u32[]{:S(2)}) collective-permute-start(bf16[4,64,1024]{2,1,0:T(8,128)(2,1)S(1)} %pad_maximum_fusion.1.refs_17_), channel_id=1, source_target_pairs={{0,15},{1,0},{2,1},{3,2},{4,3},{5,4},{6,5},{7,6},{8,7},{9,8},{10,9... | collective-permute-start | bytes 1572872 | tf_op jit(solution)/shard_map/ppermute | solution.py:28
  40.8 14.2 %collective-permute-start.24 = (bf16[4,64,1024]{2,1,0:T(8,128)(2,1)S(1)}, bf16[4,64,1024]{2,1,0:T(8,128)(2,1)S(1)}, u32[]{:S(2)}, u32[]{:S(2)}) collective-permute-start(bf16[4,64,1024]{2,1,0:T(8,128)(2,1)S(1)} %pad_maximum_fusion.1.refs_17_), channel_id=1, source_target_pairs={{0,16},{16,0},{32,48},{48,32},{64,80},{80,64},{96,112},{112,96},{1... | collective-permute-start | bytes 1572872 | tf_op jit(solution)/shard_map/ppermute | solution.py:23
  42.3 20.7 %collective-permute-start.17 = (bf16[4,64,1024]{2,1,0:T(8,128)(2,1)S(1)}, bf16[4,64,1024]{2,1,0:T(8,128)(2,1)}, u32[]{:S(2)}, u32[]{:S(2)}) collective-permute-start(bf16[4,64,1024]{2,1,0:T(8,128)(2,1)S(1)} %pad_maximum_fusion.1.refs_17_), channel_id=1, source_target_pairs={{0,1},{1,2},{2,3},{3,4},{4,5},{5,6},{6,7},{7,8},{8,9},{9,10},{10,1... | collective-permute-start | bytes 1572872 | tf_op jit(solution)/shard_map/ppermute | solution.py:28
  51.7 11.3 %collective-permute-start.29 = (bf16[4,64,1024]{2,1,0:T(8,128)(2,1)S(1)}, bf16[4,64,1024]{2,1,0:T(8,128)(2,1)S(1)}, u32[]{:S(2)}, u32[]{:S(2)}) collective-permute-start(bf16[4,64,1024]{2,1,0:T(8,128)(2,1)S(1)} %collective-permute-done.25.refs_20_), channel_id=1, source_target_pairs={{0,15},{1,0},{2,1},{3,2},{4,3},{5,4},{6,5},{7,6},{8,7},{9,8},{10,9... | collective-permute-start | bytes 1572872 | tf_op jit(solution)/shard_map/ppermute | solution.py:28
  51.7 14.0 %collective-permute-start.27 = (bf16[4,64,1024]{2,1,0:T(8,128)(2,1)S(1)}, bf16[4,64,1024]{2,1,0:T(8,128)(2,1)S(1)}, u32[]{:S(2)}, u32[]{:S(2)}) collective-permute-start(bf16[4,64,1024]{2,1,0:T(8,128)(2,1)S(1)} %collective-permute-done.25.refs_20_), channel_id=1, source_target_pairs={{0,16},{16,0},{32,48},{48,32},{64,80},{80,64},{96,112},{112,96},{1... | collective-permute-start | bytes 1572872 | tf_op jit(solution)/shard_map/ppermute | solution.py:23
  55.0 10.7 %collective-permute-start.21 = (bf16[4,64,1024]{2,1,0:T(8,128)(2,1)S(1)}, bf16[4,64,1024]{2,1,0:T(8,128)(2,1)S(1)}, u32[]{:S(2)}, u32[]{:S(2)}) collective-permute-start(bf16[4,64,1024]{2,1,0:T(8,128)(2,1)S(1)} %collective-permute-done.11.refs_12_), channel_id=1, source_target_pairs={{0,16},{16,0},{32,48},{48,32},{64,80},{80,64},{96,112},{112,96},{1... | collective-permute-start | bytes 1572872 | tf_op jit(solution)/shard_map/ppermute | solution.py:23
  55.8 18.5 %collective-permute-start.12 = (bf16[4,64,1024]{2,1,0:T(8,128)(2,1)S(1)}, bf16[4,64,1024]{2,1,0:T(8,128)(2,1)}, u32[]{:S(2)}, u32[]{:S(2)}) collective-permute-start(bf16[4,64,1024]{2,1,0:T(8,128)(2,1)S(1)} %collective-permute-done.11.refs_12_), channel_id=1, source_target_pairs={{0,1},{1,2},{2,3},{3,4},{4,5},{5,6},{6,7},{7,8},{8,9},{9,10},{10,1... | collective-permute-start | bytes 1572872 | tf_op jit(solution)/shard_map/ppermute | solution.py:28
  63.0 11.2 %collective-permute-start.1 = (bf16[2,64,1024]{2,1,0:T(8,128)(2,1)S(1)}, bf16[2,64,1024]{2,1,0:T(8,128)(2,1)S(1)}, u32[]{:S(2)}, u32[]{:S(2)}) collective-permute-start(bf16[2,64,1024]{2,1,0:T(8,128)(2,1)S(1)} %get-tuple-element.14), channel_id=1, source_target_pairs={{0,32},{16,48},{32,64},{48,80},{64,96},{80,112},{96,128},{112,144}... | collective-permute-start | bytes 786440 | tf_op jit(solution)/shard_map/ppermute | solution.py:18
  63.0 11.3 %collective-permute-start.2 = (bf16[2,64,1024]{2,1,0:T(8,128)(2,1)S(1)}, bf16[2,64,1024]{2,1,0:T(8,128)(2,1)S(1)}, u32[]{:S(2)}, u32[]{:S(2)}) collective-permute-start(bf16[2,64,1024]{2,1,0:T(8,128)(2,1)S(1)} %get-tuple-element.15), channel_id=1, source_target_pairs={{0,224},{16,240},{32,0},{48,16},{64,32},{80,48},{96,64},{112,80},{... | collective-permute-start | bytes 786440 | tf_op jit(solution)/shard_map/ppermute | solution.py:18
  65.7 16.4 %collective-permute-start.3 = (bf16[2,64,1024]{2,1,0:T(8,128)(2,1)S(1)}, bf16[2,64,1024]{2,1,0:T(8,128)(2,1)S(1)}, u32[]{:S(2)}, u32[]{:S(2)}) collective-permute-start(bf16[2,64,1024]{2,1,0:T(8,128)(2,1)S(1)} %get-tuple-element.16), channel_id=1, source_target_pairs={{0,64},{16,80},{32,96},{48,112},{64,128},{80,144},{96,160},{112,17... | collective-permute-start | bytes 786440 | tf_op jit(solution)/shard_map/ppermute | solution.py:18
  65.7 16.4 %collective-permute-start.4 = (bf16[2,64,1024]{2,1,0:T(8,128)(2,1)S(1)}, bf16[2,64,1024]{2,1,0:T(8,128)(2,1)S(1)}, u32[]{:S(2)}, u32[]{:S(2)}) collective-permute-start(bf16[2,64,1024]{2,1,0:T(8,128)(2,1)S(1)} %get-tuple-element.17), channel_id=1, source_target_pairs={{0,192},{16,208},{32,224},{48,240},{64,0},{80,16},{96,32},{112,48}... | collective-permute-start | bytes 786440 | tf_op jit(solution)/shard_map/ppermute | solution.py:18
  74.2 17.4 %collective-permute-start.5 = (bf16[2,64,1024]{2,1,0:T(8,128)(2,1)S(1)}, bf16[2,64,1024]{2,1,0:T(8,128)(2,1)S(1)}, u32[]{:S(2)}, u32[]{:S(2)}) collective-permute-start(bf16[2,64,1024]{2,1,0:T(8,128)(2,1)S(1)} %get-tuple-element.18), channel_id=1, source_target_pairs={{0,96},{16,112},{32,128},{48,144},{64,160},{80,176},{96,192},{112,... | collective-permute-start | bytes 786440 | tf_op jit(solution)/shard_map/ppermute | solution.py:18
  74.2 36.3 %collective-permute-start.30 = (bf16[4,64,1024]{2,1,0:T(8,128)(2,1)S(1)}, bf16[4,64,1024]{2,1,0:T(8,128)(2,1)}, u32[]{:S(2)}, u32[]{:S(2)}) collective-permute-start(bf16[4,64,1024]{2,1,0:T(8,128)(2,1)S(1)} %collective-permute-done.26.refs_21_), channel_id=1, source_target_pairs={{0,15},{1,0},{2,1},{3,2},{4,3},{5,4},{6,5},{7,6},{8,7},{9,8},{10,9... | collective-permute-start | bytes 1572872 | tf_op jit(solution)/shard_map/ppermute | solution.py:28
  74.4 36.3 %collective-permute-start.28 = (bf16[4,64,1024]{2,1,0:T(8,128)(2,1)S(1)}, bf16[4,64,1024]{2,1,0:T(8,128)(2,1)S(1)}, u32[]{:S(2)}, u32[]{:S(2)}) collective-permute-start(bf16[4,64,1024]{2,1,0:T(8,128)(2,1)S(1)} %collective-permute-done.26.refs_21_), channel_id=1, source_target_pairs={{0,16},{16,0},{32,48},{48,32},{64,80},{80,64},{96,112},{112,96},{1... | collective-permute-start | bytes 1572872 | tf_op jit(solution)/shard_map/ppermute | solution.py:23
  82.1 29.1 %collective-permute-start.18 = (bf16[4,64,1024]{2,1,0:T(8,128)(2,1)}, bf16[4,64,1024]{2,1,0:T(8,128)(2,1)}, u32[]{:S(2)}, u32[]{:S(2)}) collective-permute-start(bf16[4,64,1024]{2,1,0:T(8,128)(2,1)} %collective-permute-done.17.refs_13_), channel_id=1, source_target_pairs={{0,1},{1,2},{2,3},{3,4},{4,5},{5,6},{6,7},{7,8},{8,9},{9,10},{10,1... | collective-permute-start | bytes 1572872 | tf_op jit(solution)/shard_map/ppermute | solution.py:28
  82.1 15.7 %collective-permute-start.6 = (bf16[2,64,1024]{2,1,0:T(8,128)(2,1)S(1)}, bf16[2,64,1024]{2,1,0:T(8,128)(2,1)S(1)}, u32[]{:S(2)}, u32[]{:S(2)}) collective-permute-start(bf16[2,64,1024]{2,1,0:T(8,128)(2,1)S(1)} %get-tuple-element.19), channel_id=1, source_target_pairs={{0,160},{16,176},{32,192},{48,208},{64,224},{80,240},{96,0},{112,1... | collective-permute-start | bytes 786440 | tf_op jit(solution)/shard_map/ppermute | solution.py:18
  91.7 16.4 %collective-permute-start.7 = (bf16[2,64,1024]{2,1,0:T(8,128)(2,1)S(1)}, bf16[2,64,1024]{2,1,0:T(8,128)(2,1)S(1)}, u32[]{:S(2)}, u32[]{:S(2)}) collective-permute-start(bf16[2,64,1024]{2,1,0:T(8,128)(2,1)S(1)} %get-tuple-element.20), channel_id=1, source_target_pairs={{0,128},{16,144},{32,160},{48,176},{64,192},{80,208},{96,224},{112... | collective-permute-start | bytes 786440 | tf_op jit(solution)/shard_map/ppermute | solution.py:18
  97.8 15.0 %collective-permute-start.22 = (bf16[4,64,1024]{2,1,0:T(8,128)(2,1)}, bf16[4,64,1024]{2,1,0:T(8,128)(2,1)}, u32[]{:S(2)}, u32[]{:S(2)}) collective-permute-start(bf16[4,64,1024]{2,1,0:T(8,128)(2,1)} %collective-permute-done.17.refs_13_), channel_id=1, source_target_pairs={{0,16},{16,0},{32,48},{48,32},{64,80},{80,64},{96,112},{112,96},{1... | collective-permute-start | bytes 1572872 | tf_op jit(solution)/shard_map/ppermute | solution.py:23
  108.1 4.7 %collective-permute-start.31 = (bf16[4,64,1024]{2,1,0:T(8,128)(2,1)S(1)}, bf16[4,64,1024]{2,1,0:T(8,128)(2,1)}, u32[]{:S(2)}, u32[]{:S(2)}) collective-permute-start(bf16[4,64,1024]{2,1,0:T(8,128)(2,1)S(1)} %collective-permute-done.29.refs_24_), channel_id=1, source_target_pairs={{0,16},{16,0},{32,48},{48,32},{64,80},{80,64},{96,112},{112,96},{1... | collective-permute-start | bytes 1572872 | tf_op jit(solution)/shard_map/ppermute | solution.py:23
  110.7 3.1 %collective-permute-start.32 = (bf16[4,64,1024]{2,1,0:T(8,128)(2,1)}, bf16[4,64,1024]{2,1,0:T(8,128)(2,1)}, u32[]{:S(2)}, u32[]{:S(2)}) collective-permute-start(bf16[4,64,1024]{2,1,0:T(8,128)(2,1)} %collective-permute-done.30.refs_25_), channel_id=1, source_target_pairs={{0,16},{16,0},{32,48},{48,32},{64,80},{80,64},{96,112},{112,96},{1... | collective-permute-start | bytes 1572872 | tf_op jit(solution)/shard_map/ppermute | solution.py:23
  125.6 39.9 %all-to-all-start.1 = ((bf16[16,64,512]{2,1,0:T(8,128)(2,1)}), bf16[16,64,512]{2,1,0:T(8,128)(2,1)S(1)}, u32[]{:S(2)}, u32[]{:S(2)}) async-start(bf16[16,64,512]{2,1,0:T(8,128)(2,1)} %bitcast.16), calls=%async_computation.1 | async-start | bytes 2097152 | tf_op jit(solution)/shard_map/all_to_all | solution.py:229
  (25 other events, 870.6 us)
